TPU v7x, 256 devices: a whole 4x4x8 slice. The times are simulated.
256 devices in a mesh: comp: 4 (over y), gx: 16 (over z_hi, x), gy: 4 (over z_lo, core).
Axes of the slice: x: 4, y: 4, z: 8 (z_hi: 4, z_lo: 2; z = z_hi * 2 + z_lo), core: 2. Of those that a mesh axis runs over, the one named last changes fastest.
Arguments:
- state: float32 [32, 256, 128, 128], P('comp', 'gx', 'gy'), may hold values from -4 to 4
- levels: int32 [256, 128], P('gx', 'gy'), may hold values from 0 to 128
- reaction: float32 [3, 8, 8], replicated, may hold values from -2 to 2
Outputs:
- new_state: float32 [32, 256, 128, 128], P('comp', 'gx', 'gy')
Inputs may be any that keep to these rules, and one draw needn't show every extreme that they name: `levels`: 0 marks a land column, 128 a column of full depth.
All inputs are finite; a program needn't handle non-finite values.
Results may differ from a plain program's by a relative error of at most 0.00018.
Values sent between devices are 32-bit elements; how exact they have to be, the bound alone decides.
A program may use at most 64 MiB of HBM per device.

v0:
```python
import jax
import jax.numpy as jnp
from jax import lax
from jax.sharding import PartitionSpec as P

ITERS = 3
time_step = 0.25
lateral_mix = 0.05
vertical_mix = 0.1
pressure_scale = 0.05
thermal_coef = 1.0
haline_coef = 0.8
coriolis_mean = 0.5
coriolis_slope = 0.5


def padded_2(cells, sides, width):
    for axis, dim in sides:
        count = lax.axis_size(axis)
        head = lax.slice_in_dim(cells, 0, width, axis=dim)
        tail = lax.slice_in_dim(cells, cells.shape[dim] - width, cells.shape[dim], axis=dim)
        cells = jnp.concatenate(
            [
                lax.ppermute(tail, axis, [(i, (i + 1) % count) for i in range(count)]),
                cells,
                lax.ppermute(head, axis, [((i + 1) % count, i) for i in range(count)]),
            ],
            axis=dim,
        )
    return cells


def padded_to(lines, length):
    spare = -lines.shape[0] % length
    if not spare:
        return lines
    return jnp.concatenate([lines, jnp.zeros((spare, *lines.shape[1:]), lines.dtype)])


def from_root(value, axis, root):
    lines = jnp.where(lax.axis_index(axis) == root, value, jnp.zeros_like(value)).reshape(
        -1, *value.shape[1:][-1:]
    )
    padded = padded_to(lines, lax.axis_size(axis))
    own = lax.psum_scatter(padded, axis, scatter_dimension=0, tiled=True)
    return lax.all_gather(own, axis, axis=0, tiled=True)[: len(lines)].reshape(value.shape)


def along(padded, axis, shift):
    count_x = padded.shape[1] - 4
    count_y = padded.shape[2] - 4
    if axis == 1:
        return padded[:, 2 + shift : 2 + shift + count_x, 2 : 2 + count_y]
    return padded[:, 2 : 2 + count_x, 2 + shift : 2 + shift + count_y]


def centered(padded, axis):
    return (
        8.0 * (along(padded, axis, 1) - along(padded, axis, -1))
        - (along(padded, axis, 2) - along(padded, axis, -2))
    ) / 12.0


def smoothing(padded, axis):
    return (
        along(padded, axis, 2)
        + along(padded, axis, -2)
        - 4.0 * (along(padded, axis, 1) + along(padded, axis, -1))
        + 6.0 * along(padded, axis, 0)
    ) / 12.0


def transport(padded, east, north):
    return (
        east * centered(padded, 1)
        + jnp.abs(east) * smoothing(padded, 1)
        + north * centered(padded, 2)
        + jnp.abs(north) * smoothing(padded, 2)
    )


def lateral(padded):
    return (
        along(padded, 1, 1)
        + along(padded, 1, -1)
        + along(padded, 2, 1)
        + along(padded, 2, -1)
        - 4.0 * along(padded, 1, 0)
    )


def vertical(center):
    column = jnp.pad(center, ((0, 0), (0, 0), (0, 0), (1, 1)))
    return column[..., 2:] + column[..., :-2] - 2.0 * center


def dynamics_step(padded, mask, latitude, accumulate):
    center = padded[:, 2:-2, 2:-2]
    east = center[0]
    north = center[1]
    moving = padded[0:4]
    density = haline_coef * padded[3] - thermal_coef * padded[2]
    pressure = (pressure_scale * accumulate(density))[None]
    tendency = (
        lateral_mix * lateral(moving)
        + vertical_mix * vertical(center[0:4])
        - transport(moving, east, north)
    )
    rotation = (coriolis_mean + coriolis_slope * latitude)[None, :, None]
    push_east = tendency[0] + rotation * north - centered(pressure, 1)[0]
    push_north = tendency[1] - rotation * east - centered(pressure, 2)[0]
    tendency = jnp.stack([push_east, push_north, tendency[2], tendency[3]])
    advanced = center[0:4] + time_step * (1.5 * tendency - 0.5 * center[4:8])
    return jnp.concatenate([advanced * mask, tendency * mask])


def tracer_step(padded, velocity, mask, coupling):
    center = padded[:, 2:-2, 2:-2]
    growth = 2.0 * jax.nn.sigmoid(velocity[2])
    reacting = growth * jnp.einsum(
        "ij,jxyz->ixyz", coupling, center, precision=lax.Precision.HIGHEST
    )
    tendency = (
        lateral_mix * lateral(padded)
        + vertical_mix * vertical(center)
        + reacting
        - transport(padded, velocity[0], velocity[1])
    )
    return (center + time_step * tendency) * mask


def per_device(state, levels, reaction):
    cells_y = state.shape[2]
    depth_count = state.shape[3]
    slot = lax.axis_index("comp")
    row_first = lax.axis_index("gy") * cells_y
    total_rows = cells_y * lax.axis_size("gy")
    depth = lax.broadcasted_iota(jnp.int32, (1, 1, depth_count), 2)
    mask = (depth < levels[:, :, None]).astype(jnp.float32)
    lower = lax.broadcasted_iota(jnp.int32, (depth_count, depth_count), 0)
    higher = lax.broadcasted_iota(jnp.int32, (depth_count, depth_count), 1)
    summing = (lower <= higher).astype(jnp.float32)
    coupling = lax.dynamic_index_in_dim(reaction, jnp.maximum(slot - 1, 0), 0, keepdims=False)

    def accumulate(density):
        return jnp.dot(density, summing, precision=lax.Precision.HIGHEST)

    def global_rows(width):
        return row_first - width + lax.iota(jnp.int32, cells_y + 2 * width)

    def latitude(width):
        rows = global_rows(width)
        return 2.0 * rows.astype(jnp.float32) / float(total_rows - 1) - 1.0

    current = state * mask[None]
    for step in range(ITERS):
        extend_padded = padded_2(current, (("gx", 1), ("gy", 2)), 2)
        inside_rows = global_rows(2)
        region_latitude = latitude(0)

        def run_dynamics(operands):
            return dynamics_step(operands[0], operands[2], region_latitude, accumulate)

        def run_tracers(operands):
            return tracer_step(operands[0], operands[1], operands[2], coupling)

        current = lax.cond(
            slot == 0,
            run_dynamics,
            run_tracers,
            (
                extend_padded
                * ((inside_rows >= 0) & (inside_rows < total_rows)).astype(jnp.float32)[
                    None, None, :, None
                ],
                from_root(current[0:3], "comp", 0),
                mask,
            ),
        )
    return current


def solution(mesh):
    in_specs = (P("comp", "gx", "gy", None), P("gx", "gy"), P())
    out_specs = P("comp", "gx", "gy", None)
    return jax.shard_map(
        per_device, mesh=mesh, in_specs=in_specs, out_specs=out_specs, check_vma=False
    )
```

profile of v0, /device:TPU:78, one launch (start us, length us, event | category | flops | bytes accessed | tf_op | source)
XLA Modules:
  0.0 169.2 jit_solution(1472869630248358750)
XLA Ops:
  6.5 0.8 fusion.99
  7.4 1.9 %broadcast_multiply_fusion = f32[8,16,32,128]{3,2,1,0:T(8,128)S(1)} fusion(f32[8,16,32,128]{3,2,1,0:T(8,128)} %param.9, f32[16,32,128]{2,1,0:T(8,128)S(1)} %fusion.99), kind=kLoop, calls=%fused_computation.174 | loop fusion | flops 524288 | bytes 4456448 | tf_op jit(solution)/shard_map/mul | solution.py:155
  9.3 1.1 slice_select_fusion.2
  10.5 4.5 %collective-permute-start = (f32[8,2,32,128]{3,2,1,0:T(8,128)S(1)}, f32[8,2,32,128]{3,2,1,0:T(8,128)S(1)}, u32[]{:S(2)}, u32[]{:S(2)}) collective-permute-start(f32[8,2,32,128]{3,2,1,0:T(8,128)S(1)} %get-tuple-element.152), channel_id=1, source_target_pairs={{0,4},{4,8},{8,12},{12,16},{16,20},{20,24},{24,28},{28,32},{32,36}... | collective-permute-start | bytes 786440 | tf_op jit(solution)/shard_map/ppermute | solution.py:24
  15.0 0.6 multiply_add_fusion.3
  15.6 10.5 %collective-permute-done = f32[8,2,32,128]{3,2,1,0:T(8,128)S(1)} collective-permute-done((f32[8,2,32,128]{3,2,1,0:T(8,128)S(1)}, f32[8,2,32,128]{3,2,1,0:T(8,128)S(1)}, u32[]{:S(2)}, u32[]{:S(2)}) %collective-permute-start) | collective-permute-done | bytes 262176 | tf_op jit(solution)/shard_map/ppermute | solution.py:24
  26.1 6.5 %collective-permute-done.1 = f32[8,2,32,128]{3,2,1,0:T(8,128)S(1)} collective-permute-done((f32[8,2,32,128]{3,2,1,0:T(8,128)S(1)}, f32[8,2,32,128]{3,2,1,0:T(8,128)S(1)}, u32[]{:S(2)}, u32[]{:S(2)}) %collective-permute-start.1) | collective-permute-done | bytes 262176 | tf_op jit(solution)/shard_map/ppermute | solution.py:26
  32.8 1.7 %collective-permute-start.3 = (f32[8,20,2,128]{3,2,1,0:T(2,128)S(1)}, f32[8,20,2,128]{3,2,1,0:T(2,128)}, u32[]{:S(2)}, u32[]{:S(2)}) collective-permute-start(f32[8,20,2,128]{3,2,1,0:T(2,128)S(1)} %get-tuple-element.147), channel_id=1, source_target_pairs={{1,0},{2,1},{3,2},{0,3},{5,4},{6,5},{7,6},{4,7},{9,8},{10,9},{11,1... | collective-permute-start | bytes 491528 | tf_op jit(solution)/shard_map/ppermute | solution.py:26
  34.6 0.6 fusion.100
  35.2 3.3 %collective-permute-done.2 = f32[8,20,2,128]{3,2,1,0:T(2,128)S(1)} collective-permute-done((f32[8,20,2,128]{3,2,1,0:T(2,128)S(1)}, f32[8,20,2,128]{3,2,1,0:T(2,128)S(1)}, u32[]{:S(2)}, u32[]{:S(2)}) %collective-permute-start.2) | collective-permute-done | bytes 163872 | tf_op jit(solution)/shard_map/ppermute | solution.py:24
  38.5 0.7 copy-done.8
  39.1 2.3 %maximum_multiply_fusion = f32[8,20,36,128]{3,2,1,0:T(8,128)S(1)} fusion(f32[8,20,2,128]{3,2,1,0:T(2,128)} %collective-permute-done.3, f32[8,2,32,128]{3,2,1,0:T(8,128)} %copy-done.7, f32[8,16,32,128]{3,2,1,0:T(8,128)} %copy-done.2, f32[8,2,32,128]{3,2,1,0:T(8,128)} %copy-done.6, f32[8,20,2,128]{3,2,1,0:T(2,128)} %copy-done.8, f32[36]{0:T(128)S(1)} %and_convert_fusion), kind=kLoop, calls=%fused_computation.171 | loop fusion | flops 3686400 | bytes 5898384 | tf_op jit(solution)/shard_map/mul | solution.py:172
  41.4 14.7 %all_gather.9 = f32[1536,128]{1,0:T(8,128)S(1)} all-gather(f32[384,128]{1,0:T(8,128)} %reduce-scatter.4.cloned.1.call-done), channel_id=1, replica_groups=mesh['comp'=4,'gx'=16,'gy'=4] {'comp'}, dimensions={0}, use_global_device_ids=true | all-gather | bytes 983040 | tf_op jit(solution)/shard_map/all_gather | solution.py:46
  56.1 8.6 %conditional.3 = (f32[8,16,32,128]{3,2,1,0:T(8,128)S(1)}) conditional(s32[]{:T(128)} %convert_element_type.41, (f32[8,20,36,128]{3,2,1,0:T(8,128)S(1)}, f32[1536,128]{1,0:T(8,128)S(1)}, f32[8,8]{1,0:T(8,128)S(1)}, f32[16,32,128]{2,1,0:T(8,128)S(1)}) %tuple.23, (f32[8,20,36,128]{3,2,1,0:T(8,128)S(1)}, f32[32]{0:T(128)S(1)}, f32[128,128]{1,0:T(8,128)}, ...), branch_computations={%region_1.2_spmd, %region_2.3_spmd} | conditional | flops 155859008 | bytes 41029640 | solution.py:167
  56.1 0.1 divide_multiply_fusion
  56.3 1.7 %copy.9 = f32[8,20,36,128]{3,0,2,1:T(8,128)S(1)} copy(f32[8,20,36,128]{3,2,1,0:T(8,128)S(1)} %get-tuple-element.91) | data formatting | bytes 5898240 | tf_op jit(solution)/shard_map
  58.1 6.1 %fusion.8 = f32[8,16,32,128]{3,0,2,1:T(8,128)S(1)} fusion(f32[8,16,32,128]{3,0,2,1:T(8,128)S(1)} %slice.582, f32[8,20,36,128]{3,0,2,1:T(8,128)S(1)} %copy.9, f32[16,32,128]{2,1,0:T(8,128)S(1)} %get-tuple-element.68, f32[16,32,128]{2,1,0:T(8,128)S(1)} %bitcast.91, f32[16,32,128]{2,1,0:T(8,128)S(1)} %bitcast.93, f32[16,32,128]{2,1,0:T(8,128)S(1)} %bitcast.90, ...), kind=kOutput, calls=%fused_computation.10 | convolution fusion | flops 72351744 | bytes 24645632 | tf_op jit(solution)/shard_map/cond/branch_0_fun/ij,jxyz->ixyz/dot_general | solution.py:120
  64.3 0.4 copy.6
  64.7 1.1 slice_select_fusion.1
  65.9 1.1 collective-permute-start.4
  67.0 1.0 collective-permute-start.5
  68.0 6.3 %collective-permute-done.4 = f32[8,2,32,128]{3,2,1,0:T(8,128)S(1)} collective-permute-done((f32[8,2,32,128]{3,2,1,0:T(8,128)S(1)}, f32[8,2,32,128]{3,2,1,0:T(8,128)S(1)}, u32[]{:S(2)}, u32[]{:S(2)}) %collective-permute-start.4) | collective-permute-done | bytes 262176 | tf_op jit(solution)/shard_map/ppermute | solution.py:24
  74.3 6.8 %collective-permute-done.5 = f32[8,2,32,128]{3,2,1,0:T(8,128)S(1)} collective-permute-done((f32[8,2,32,128]{3,2,1,0:T(8,128)S(1)}, f32[8,2,32,128]{3,2,1,0:T(8,128)S(1)}, u32[]{:S(2)}, u32[]{:S(2)}) %collective-permute-start.5) | collective-permute-done | bytes 262176 | tf_op jit(solution)/shard_map/ppermute | solution.py:26
  81.4 1.7 %collective-permute-start.7 = (f32[8,20,2,128]{3,2,1,0:T(2,128)S(1)}, f32[8,20,2,128]{3,2,1,0:T(2,128)S(1)}, u32[]{:S(2)}, u32[]{:S(2)}) collective-permute-start(f32[8,20,2,128]{3,2,1,0:T(2,128)S(1)} %get-tuple-element.145), channel_id=1, source_target_pairs={{1,0},{2,1},{3,2},{0,3},{5,4},{6,5},{7,6},{4,7},{9,8},{10,9},{11,1... | collective-permute-start | bytes 491528 | tf_op jit(solution)/shard_map/ppermute | solution.py:26
  83.1 4.7 %collective-permute-done.6 = f32[8,20,2,128]{3,2,1,0:T(2,128)S(1)} collective-permute-done((f32[8,20,2,128]{3,2,1,0:T(2,128)S(1)}, f32[8,20,2,128]{3,2,1,0:T(2,128)S(1)}, u32[]{:S(2)}, u32[]{:S(2)}) %collective-permute-start.6) | collective-permute-done | bytes 163872 | tf_op jit(solution)/shard_map/ppermute | solution.py:24
  87.8 2.1 %maximum_multiply_fusion.1 = f32[8,20,36,128]{3,2,1,0:T(8,128)S(1)} fusion(f32[8,20,2,128]{3,2,1,0:T(2,128)S(1)} %collective-permute-done.7, f32[8,2,32,128]{3,2,1,0:T(8,128)S(1)} %collective-permute-done.5, f32[8,16,32,128]{3,2,1,0:T(8,128)} %copy-done.3, f32[8,2,32,128]{3,2,1,0:T(8,128)S(1)} %collective-permute-done.4, ...), kind=kLoop, calls=%fused_computation.172 | loop fusion | flops 3686400 | bytes 5898384 | tf_op jit(solution)/shard_map/mul | solution.py:172
  90.0 14.8 %all_gather.10 = f32[1536,128]{1,0:T(8,128)S(1)} all-gather(f32[384,128]{1,0:T(8,128)} %reduce-scatter.6.cloned.1.call-done), channel_id=1, replica_groups=mesh['comp'=4,'gx'=16,'gy'=4] {'comp'}, dimensions={0}, use_global_device_ids=true | all-gather | bytes 983040 | tf_op jit(solution)/shard_map/all_gather | solution.py:46
  104.8 8.6 %conditional.4 = (f32[8,16,32,128]{3,2,1,0:T(8,128)S(1)}) conditional(s32[]{:T(128)} %convert_element_type.41, (f32[8,20,36,128]{3,2,1,0:T(8,128)S(1)}, f32[1536,128]{1,0:T(8,128)S(1)}, f32[8,8]{1,0:T(8,128)S(1)}, f32[16,32,128]{2,1,0:T(8,128)S(1)}) %tuple.25, (f32[8,20,36,128]{3,2,1,0:T(8,128)S(1)}, f32[32]{0:T(128)S(1)}, f32[128,128]{1,0:T(8,128)}, ...), branch_computations={%region_4.5_spmd, %region_5.6_spmd} | conditional | flops 155859008 | bytes 41029640 | solution.py:167
  104.8 0.1 divide_multiply_fusion.1
  104.9 1.7 %copy.10 = f32[8,20,36,128]{3,0,2,1:T(8,128)S(1)} copy(f32[8,20,36,128]{3,2,1,0:T(8,128)S(1)} %get-tuple-element.95) | data formatting | bytes 5898240 | tf_op jit(solution)/shard_map
  106.8 6.1 %fusion.41 = f32[8,16,32,128]{3,0,2,1:T(8,128)S(1)} fusion(f32[8,16,32,128]{3,0,2,1:T(8,128)S(1)} %slice.602, f32[8,20,36,128]{3,0,2,1:T(8,128)S(1)} %copy.10, f32[16,32,128]{2,1,0:T(8,128)S(1)} %get-tuple-element.76, f32[16,32,128]{2,1,0:T(8,128)S(1)} %bitcast.96, f32[16,32,128]{2,1,0:T(8,128)S(1)} %bitcast.98, f32[16,32,128]{2,1,0:T(8,128)S(1)} %bitcast.95, ...), kind=kOutput, calls=%fused_computation.67 | convolution fusion | flops 72351744 | bytes 24645632 | tf_op jit(solution)/shard_map/cond/branch_0_fun/ij,jxyz->ixyz/dot_general | solution.py:120
  112.9 0.4 copy.7
  113.3 1.1 slice_select_fusion
  114.6 2.0 %collective-permute-start.9 = (f32[8,2,32,128]{3,2,1,0:T(8,128)S(1)}, f32[8,2,32,128]{3,2,1,0:T(8,128)S(1)}, u32[]{:S(2)}, u32[]{:S(2)}) collective-permute-start(f32[8,2,32,128]{3,2,1,0:T(8,128)S(1)} %get-tuple-element.149), channel_id=1, source_target_pairs={{4,0},{8,4},{12,8},{16,12},{20,16},{24,20},{28,24},{32,28},{36,32}... | collective-permute-start | bytes 786440 | tf_op jit(solution)/shard_map/ppermute | solution.py:26
  116.6 6.1 %collective-permute-done.8 = f32[8,2,32,128]{3,2,1,0:T(8,128)S(1)} collective-permute-done((f32[8,2,32,128]{3,2,1,0:T(8,128)S(1)}, f32[8,2,32,128]{3,2,1,0:T(8,128)S(1)}, u32[]{:S(2)}, u32[]{:S(2)}) %collective-permute-start.8) | collective-permute-done | bytes 262176 | tf_op jit(solution)/shard_map/ppermute | solution.py:24
  122.7 6.2 %collective-permute-done.9 = f32[8,2,32,128]{3,2,1,0:T(8,128)S(1)} collective-permute-done((f32[8,2,32,128]{3,2,1,0:T(8,128)S(1)}, f32[8,2,32,128]{3,2,1,0:T(8,128)S(1)}, u32[]{:S(2)}, u32[]{:S(2)}) %collective-permute-start.9) | collective-permute-done | bytes 262176 | tf_op jit(solution)/shard_map/ppermute | solution.py:26
  129.1 1.7 %collective-permute-start.11 = (f32[8,20,2,128]{3,2,1,0:T(2,128)S(1)}, f32[8,20,2,128]{3,2,1,0:T(2,128)S(1)}, u32[]{:S(2)}, u32[]{:S(2)}) collective-permute-start(f32[8,20,2,128]{3,2,1,0:T(2,128)S(1)} %get-tuple-element.143), channel_id=1, source_target_pairs={{1,0},{2,1},{3,2},{0,3},{5,4},{6,5},{7,6},{4,7},{9,8},{10,9},{11,1... | collective-permute-start | bytes 491528 | tf_op jit(solution)/shard_map/ppermute | solution.py:26
  130.9 3.0 %collective-permute-done.10 = f32[8,20,2,128]{3,2,1,0:T(2,128)S(1)} collective-permute-done((f32[8,20,2,128]{3,2,1,0:T(2,128)S(1)}, f32[8,20,2,128]{3,2,1,0:T(2,128)S(1)}, u32[]{:S(2)}, u32[]{:S(2)}) %collective-permute-start.10) | collective-permute-done | bytes 163872 | tf_op jit(solution)/shard_map/ppermute | solution.py:24
  133.8 1.5 collective-permute-done.11
  135.3 2.1 %maximum_multiply_fusion.2 = f32[8,20,36,128]{3,2,1,0:T(8,128)S(1)} fusion(f32[8,20,2,128]{3,2,1,0:T(2,128)S(1)} %collective-permute-done.11, f32[8,2,32,128]{3,2,1,0:T(8,128)S(1)} %collective-permute-done.9, f32[8,16,32,128]{3,2,1,0:T(8,128)} %copy-done.4, f32[8,2,32,128]{3,2,1,0:T(8,128)S(1)} %collective-permute-done.8, ...), kind=kLoop, calls=%fused_computation.173 | loop fusion | flops 3686400 | bytes 5898384 | tf_op jit(solution)/shard_map/mul | solution.py:172
  137.5 14.5 %all_gather.11 = f32[1536,128]{1,0:T(8,128)S(1)} all-gather(f32[384,128]{1,0:T(8,128)} %reduce-scatter.8.cloned.1.call-done), channel_id=1, replica_groups=mesh['comp'=4,'gx'=16,'gy'=4] {'comp'}, dimensions={0}, use_global_device_ids=true | all-gather | bytes 983040 | tf_op jit(solution)/shard_map/all_gather | solution.py:46
  152.0 8.6 %conditional.5 = (f32[8,16,32,128]{3,2,1,0:T(8,128)S(1)}) conditional(s32[]{:T(128)} %convert_element_type.41, (f32[8,20,36,128]{3,2,1,0:T(8,128)S(1)}, f32[1536,128]{1,0:T(8,128)S(1)}, f32[8,8]{1,0:T(8,128)S(1)}, f32[16,32,128]{2,1,0:T(8,128)S(1)}) %tuple.27, (f32[8,20,36,128]{3,2,1,0:T(8,128)S(1)}, f32[32]{0:T(128)S(1)}, f32[128,128]{1,0:T(8,128)}, ...), branch_computations={%region_7.8_spmd, %region_8.9_spmd} | conditional | flops 155859008 | bytes 41029640 | solution.py:167
  152.0 0.1 divide_multiply_fusion.2
  152.2 1.7 %copy.11 = f32[8,20,36,128]{3,0,2,1:T(8,128)S(1)} copy(f32[8,20,36,128]{3,2,1,0:T(8,128)S(1)} %get-tuple-element.99) | data formatting | bytes 5898240 | tf_op jit(solution)/shard_map
  154.0 6.1 %fusion.74 = f32[8,16,32,128]{3,0,2,1:T(8,128)S(1)} fusion(f32[8,16,32,128]{3,0,2,1:T(8,128)S(1)} %slice.622, f32[8,20,36,128]{3,0,2,1:T(8,128)S(1)} %copy.11, f32[16,32,128]{2,1,0:T(8,128)S(1)} %get-tuple-element.84, f32[16,32,128]{2,1,0:T(8,128)S(1)} %bitcast.101, f32[16,32,128]{2,1,0:T(8,128)S(1)} %bitcast.103, f32[16,32,128]{2,1,0:T(8,128)S(1)} %bitcast.100, ...), kind=kOutput, calls=%fused_computation.124 | convolution fusion | flops 72351744 | bytes 24645632 | tf_op jit(solution)/shard_map/cond/branch_0_fun/ij,jxyz->ixyz/dot_general | solution.py:120
  160.2 0.4 copy.8
  160.6 1.3 copy-done.5
  161.9 0.7 copy-done.1
  (44 shorter events, 1.5 us)
Async XLA Ops:
  6.5 9.1 %copy-start = (f32[3,8,8]{2,1,0:T(8,128)S(1)}, f32[3,8,8]{2,1,0:T(8,128)}, u32[]{:S(2)}) copy-start(f32[3,8,8]{2,1,0:T(8,128)} %param.11) | copy-start | bytes 2308
  6.5 34.9 %reduce-scatter.4.cloned.1.call-start = ((), (), s32[]{:S(2)}) async-start(), calls=%async_computation.3 | async-start | bytes 983040 | tf_op jit(solution)/shard_map/reduce_scatter | solution.py:45
  9.3 23.4 %copy-start.2 = (f32[8,16,32,128]{3,2,1,0:T(8,128)}, f32[8,16,32,128]{3,2,1,0:T(8,128)S(1)}, u32[]{:S(2)}) copy-start(f32[8,16,32,128]{3,2,1,0:T(8,128)S(1)} %broadcast_multiply_fusion) | copy-start | bytes 6291460
  10.4 79.5 %reduce-scatter.6.cloned.1.call-start = ((), (), s32[]{:S(2)}) async-start(), calls=%async_computation.4 | async-start | bytes 983040 | tf_op jit(solution)/shard_map/reduce_scatter | solution.py:45
  10.5 15.6 %collective-permute-start = (f32[8,2,32,128]{3,2,1,0:T(8,128)S(1)}, f32[8,2,32,128]{3,2,1,0:T(8,128)S(1)}, u32[]{:S(2)}, u32[]{:S(2)}) collective-permute-start(f32[8,2,32,128]{3,2,1,0:T(8,128)S(1)} %get-tuple-element.152), channel_id=1, source_target_pairs={{0,4},{4,8},{8,12},{12,16},{16,20},{20,24},{24,28},{28,32},{32,36}... | collective-permute-start | bytes 786440 | tf_op jit(solution)/shard_map/ppermute | solution.py:24
  15.0 17.6 %collective-permute-start.1 = (f32[8,2,32,128]{3,2,1,0:T(8,128)S(1)}, f32[8,2,32,128]{3,2,1,0:T(8,128)S(1)}, u32[]{:S(2)}, u32[]{:S(2)}) collective-permute-start(f32[8,2,32,128]{3,2,1,0:T(8,128)S(1)} %get-tuple-element.153), channel_id=1, source_target_pairs={{4,0},{8,4},{12,8},{16,12},{20,16},{24,20},{28,24},{32,28},{36,32}... | collective-permute-start | bytes 786440 | tf_op jit(solution)/shard_map/ppermute | solution.py:26
  26.1 12.4 %copy-start.6 = (f32[8,2,32,128]{3,2,1,0:T(8,128)}, f32[8,2,32,128]{3,2,1,0:T(8,128)S(1)}, u32[]{:S(2)}) copy-start(f32[8,2,32,128]{3,2,1,0:T(8,128)S(1)} %collective-permute-done) | copy-start | bytes 786436
  32.6 5.9 %copy-start.7 = (f32[8,2,32,128]{3,2,1,0:T(8,128)}, f32[8,2,32,128]{3,2,1,0:T(8,128)S(1)}, u32[]{:S(2)}) copy-start(f32[8,2,32,128]{3,2,1,0:T(8,128)S(1)} %collective-permute-done.1) | copy-start | bytes 786436
  32.7 5.7 %collective-permute-start.2 = (f32[8,20,2,128]{3,2,1,0:T(2,128)S(1)}, f32[8,20,2,128]{3,2,1,0:T(2,128)S(1)}, u32[]{:S(2)}, u32[]{:S(2)}) collective-permute-start(f32[8,20,2,128]{3,2,1,0:T(2,128)S(1)} %get-tuple-element.146), channel_id=1, source_target_pairs={{0,1},{1,2},{2,3},{3,0},{4,5},{5,6},{6,7},{7,4},{8,9},{9,10},{10,1... | collective-permute-start | bytes 491528 | tf_op jit(solution)/shard_map/ppermute | solution.py:24
  32.8 6.3 %collective-permute-start.3 = (f32[8,20,2,128]{3,2,1,0:T(2,128)S(1)}, f32[8,20,2,128]{3,2,1,0:T(2,128)}, u32[]{:S(2)}, u32[]{:S(2)}) collective-permute-start(f32[8,20,2,128]{3,2,1,0:T(2,128)S(1)} %get-tuple-element.147), channel_id=1, source_target_pairs={{1,0},{2,1},{3,2},{0,3},{5,4},{6,5},{7,6},{4,7},{9,8},{10,9},{11,1... | collective-permute-start | bytes 491528 | tf_op jit(solution)/shard_map/ppermute | solution.py:26
  35.2 20.9 %copy-start.9 = (f32[32]{0:T(128)S(1)}, f32[32]{0:T(128)}, u32[]{:S(2)}) copy-start(f32[32]{0:T(128)} %multiply_add_fusion.3) | copy-start | bytes 388
  38.5 0.7 copy-start.8
  64.7 16.6 %copy-start.3 = (f32[8,16,32,128]{3,2,1,0:T(8,128)}, f32[8,16,32,128]{3,2,1,0:T(8,128)S(1)}, u32[]{:S(2)}) copy-start(f32[8,16,32,128]{3,2,1,0:T(8,128)S(1)} %get-tuple-element.156) | copy-start | bytes 6291460
  65.8 71.6 %reduce-scatter.8.cloned.1.call-start = ((), (), s32[]{:S(2)}) async-start(), calls=%async_computation.5 | async-start | bytes 983040 | tf_op jit(solution)/shard_map/reduce_scatter | solution.py:45
  65.9 8.4 %collective-permute-start.4 = (f32[8,2,32,128]{3,2,1,0:T(8,128)S(1)}, f32[8,2,32,128]{3,2,1,0:T(8,128)S(1)}, u32[]{:S(2)}, u32[]{:S(2)}) collective-permute-start(f32[8,2,32,128]{3,2,1,0:T(8,128)S(1)} %get-tuple-element.150), channel_id=1, source_target_pairs={{0,4},{4,8},{8,12},{12,16},{16,20},{20,24},{24,28},{28,32},{32,36}... | collective-permute-start | bytes 786440 | tf_op jit(solution)/shard_map/ppermute | solution.py:24
  67.0 14.2 %collective-permute-start.5 = (f32[8,2,32,128]{3,2,1,0:T(8,128)S(1)}, f32[8,2,32,128]{3,2,1,0:T(8,128)S(1)}, u32[]{:S(2)}, u32[]{:S(2)}) collective-permute-start(f32[8,2,32,128]{3,2,1,0:T(8,128)S(1)} %get-tuple-element.151), channel_id=1, source_target_pairs={{4,0},{8,4},{12,8},{16,12},{20,16},{24,20},{28,24},{32,28},{36,32}... | collective-permute-start | bytes 786440 | tf_op jit(solution)/shard_map/ppermute | solution.py:26
  81.3 6.5 %collective-permute-start.6 = (f32[8,20,2,128]{3,2,1,0:T(2,128)S(1)}, f32[8,20,2,128]{3,2,1,0:T(2,128)S(1)}, u32[]{:S(2)}, u32[]{:S(2)}) collective-permute-start(f32[8,20,2,128]{3,2,1,0:T(2,128)S(1)} %get-tuple-element.144), channel_id=1, source_target_pairs={{0,1},{1,2},{2,3},{3,0},{4,5},{5,6},{6,7},{7,4},{8,9},{9,10},{10,1... | collective-permute-start | bytes 491528 | tf_op jit(solution)/shard_map/ppermute | solution.py:24
  81.4 6.4 %collective-permute-start.7 = (f32[8,20,2,128]{3,2,1,0:T(2,128)S(1)}, f32[8,20,2,128]{3,2,1,0:T(2,128)S(1)}, u32[]{:S(2)}, u32[]{:S(2)}) collective-permute-start(f32[8,20,2,128]{3,2,1,0:T(2,128)S(1)} %get-tuple-element.145), channel_id=1, source_target_pairs={{1,0},{2,1},{3,2},{0,3},{5,4},{6,5},{7,6},{4,7},{9,8},{10,9},{11,1... | collective-permute-start | bytes 491528 | tf_op jit(solution)/shard_map/ppermute | solution.py:26
  113.3 15.7 %copy-start.4 = (f32[8,16,32,128]{3,2,1,0:T(8,128)}, f32[8,16,32,128]{3,2,1,0:T(8,128)S(1)}, u32[]{:S(2)}) copy-start(f32[8,16,32,128]{3,2,1,0:T(8,128)S(1)} %get-tuple-element.157) | copy-start | bytes 6291460
  114.5 8.2 %collective-permute-start.8 = (f32[8,2,32,128]{3,2,1,0:T(8,128)S(1)}, f32[8,2,32,128]{3,2,1,0:T(8,128)S(1)}, u32[]{:S(2)}, u32[]{:S(2)}) collective-permute-start(f32[8,2,32,128]{3,2,1,0:T(8,128)S(1)} %get-tuple-element.148), channel_id=1, source_target_pairs={{0,4},{4,8},{8,12},{12,16},{16,20},{20,24},{24,28},{28,32},{32,36}... | collective-permute-start | bytes 786440 | tf_op jit(solution)/shard_map/ppermute | solution.py:24
  114.6 14.3 %collective-permute-start.9 = (f32[8,2,32,128]{3,2,1,0:T(8,128)S(1)}, f32[8,2,32,128]{3,2,1,0:T(8,128)S(1)}, u32[]{:S(2)}, u32[]{:S(2)}) collective-permute-start(f32[8,2,32,128]{3,2,1,0:T(8,128)S(1)} %get-tuple-element.149), channel_id=1, source_target_pairs={{4,0},{8,4},{12,8},{16,12},{20,16},{24,20},{28,24},{32,28},{36,32}... | collective-permute-start | bytes 786440 | tf_op jit(solution)/shard_map/ppermute | solution.py:26
  129.0 4.8 %collective-permute-start.10 = (f32[8,20,2,128]{3,2,1,0:T(2,128)S(1)}, f32[8,20,2,128]{3,2,1,0:T(2,128)S(1)}, u32[]{:S(2)}, u32[]{:S(2)}) collective-permute-start(f32[8,20,2,128]{3,2,1,0:T(2,128)S(1)} %get-tuple-element.142), channel_id=1, source_target_pairs={{0,1},{1,2},{2,3},{3,0},{4,5},{5,6},{6,7},{7,4},{8,9},{9,10},{10,1... | collective-permute-start | bytes 491528 | tf_op jit(solution)/shard_map/ppermute | solution.py:24
  129.1 6.2 %collective-permute-start.11 = (f32[8,20,2,128]{3,2,1,0:T(2,128)S(1)}, f32[8,20,2,128]{3,2,1,0:T(2,128)S(1)}, u32[]{:S(2)}, u32[]{:S(2)}) collective-permute-start(f32[8,20,2,128]{3,2,1,0:T(2,128)S(1)} %get-tuple-element.143), channel_id=1, source_target_pairs={{1,0},{2,1},{3,2},{0,3},{5,4},{6,5},{7,6},{4,7},{9,8},{10,9},{11,1... | collective-permute-start | bytes 491528 | tf_op jit(solution)/shard_map/ppermute | solution.py:26
  160.6 1.3 copy-start.5
  161.9 0.7 copy-start.1
Sparse Core Ops, SparseCore 0:
  10.6 24.9 reduce-scatter.3
  65.9 20.7 reduce-scatter.5
  114.6 21.2 reduce-scatter.7
where the time goes:
time: 170 us; the launch traced here: 169 us
  waiting for transfers between devices  55 us (32%)
  blocking collectives  44 us (26%)
  matrix products  18.4 us (11%)
  other arithmetic  14.5 us (9%)
  starting transfers between devices  14.2 us (8%)
  between operations  13.3 us (8%)
  local copies, waits for them, and re-layouts  9.62 us (6%)
    all_gather x3, blocking collectives, from_root(): lax.all_gather(own, axis, axis=0, tiled=True)[:len(lines)]  44 us
    ppermute x6, waiting for transfers between devices, padded_2(): lax.ppermute(tail, axis, [(i, (i + 1) % count) for i in range(count)])  33.8 us
    ppermute x6, waiting for transfers between devices, padded_2(): lax.ppermute(head, axis, [((i + 1) % count, i) for i in range(count)])  21.1 us
    dot_general x3, matrix products, tracer_step(): jnp.einsum('ij,jxyz->ixyz', coupling, center, precision=lax.Precision.HIG...  18.4 us
    ppermute x6, starting transfers between devices, padded_2(): lax.ppermute(head, axis, [((i + 1) % count, i) for i in range(count)])  8.25 us
    mul x3, other arithmetic, per_device(): extend_padded * ((inside_rows >= 0) & (inside_rows < total_rows)).astype(...  6.49 us
    ppermute x6, starting transfers between devices, padded_2(): lax.ppermute(tail, axis, [(i, (i + 1) % count) for i in range(count)])  5.88 us
    another operation x3, local copies, waits for them, and re-layouts  5.13 us
  transfers between devices with their start and end apart: 15, of which 10 were waited for; matrix products, arithmetic and copies ran while one was open for 5% of the time, Pallas kernels for 0%

commit v1 on v0

--- a/solution.py
+++ b/solution.py
@@ -2,6 +2,7 @@
 import jax.numpy as jnp
 from jax import lax
 from jax.sharding import PartitionSpec as P
+from jax.lax import all_to_all, axis_size
 
 ITERS = 3
 time_step = 0.25
@@ -43,7 +44,9 @@
     )
     padded = padded_to(lines, lax.axis_size(axis))
     own = lax.psum_scatter(padded, axis, scatter_dimension=0, tiled=True)
-    return lax.all_gather(own, axis, axis=0, tiled=True)[: len(lines)].reshape(value.shape)
+    return jnp.concatenate(all_to_all(jnp.stack([own] * axis_size(axis)), axis, 0, 0), axis=0)[
+        : len(lines)
+    ].reshape(value.shape)
 
 
 def along(padded, axis, shift):

time: 170 us -> 179 us (1.053)
  blocking collectives: 44 us -> 0 us
  starting transfers between devices: 14.2 us -> 38.2 us
  waiting for transfers between devices: 55 us -> 74.2 us
  local copies, waits for them, and re-layouts: 9.62 us -> 15.2 us
  other arithmetic: 14.5 us -> 18 us
    reduce_scatter x3, waiting for transfers between devices: 0.06 us -> 60.7 us  [from_root(): own = lax.psum_scatter(padded, axis, scatter_dimension=0, tiled=True)]
    all_gather x3 -> x0, blocking collectives: 44 us -> none  [from_root(): lax.all_gather(own, axis, axis=0, tiled=True)[:len(lines)]]
    ppermute x6, waiting for transfers between devices: 33.8 us -> 8.36 us  [padded_2(): lax.ppermute(tail, axis, [(i, (i + 1) % count) for i in range(count)])]
    all_to_all x0 -> x3, starting transfers between devices: none -> 20.9 us  [from_root(): all_to_all(jnp.stack([own] * axis_size(axis)), axis, 0, 0)]
    ppermute x6, waiting for transfers between devices: 21.1 us -> 1.82 us  [padded_2(): lax.ppermute(head, axis, [((i + 1) % count, i) for i in range(count)])]
    ppermute x6, starting transfers between devices: 5.88 us -> 12 us  [padded_2(): lax.ppermute(tail, axis, [(i, (i + 1) % count) for i in range(count)])]
    another operation x3 -> x6, local copies, waits for them, and re-layouts: 5.13 us -> 10.7 us  [the longest x3 5.58 us: from_root(): jnp.stack([own] * axis_size(axis))]
    mul x3, other arithmetic: 0.44 us -> 3.86 us  [tracer_step(): growth * jnp.einsum('ij,jxyz->ixyz', coupling, center, precision=lax.Prec...]
  transfers between devices with their start and end apart: 15 -> 18, of which waited for: 10 -> 12; matrix products, arithmetic and copies ran while one was open for 5% -> 8% of each run, Pallas kernels for 0% -> 0%
where the time goes in v1:
time: 179 us; the launch traced here: 177 us
  waiting for transfers between devices  74.2 us (41%)
  starting transfers between devices  38.2 us (21%)
  matrix products  18.4 us (10%)
  other arithmetic  18 us (10%)
  local copies, waits for them, and re-layouts  15.2 us (8%)
  between operations  13.3 us (7%)
    reduce_scatter x3, waiting for transfers between devices, from_root(): own = lax.psum_scatter(padded, axis, scatter_dimension=0, tiled=True)  60.7 us
    all_to_all x3, starting transfers between devices, from_root(): all_to_all(jnp.stack([own] * axis_size(axis)), axis, 0, 0)  20.9 us
    dot_general x3, matrix products, tracer_step(): jnp.einsum('ij,jxyz->ixyz', coupling, center, precision=lax.Precision.HIG...  18.4 us
    ppermute x6, starting transfers between devices, padded_2(): lax.ppermute(tail, axis, [(i, (i + 1) % count) for i in range(count)])  12 us
    ppermute x6, waiting for transfers between devices, padded_2(): lax.ppermute(tail, axis, [(i, (i + 1) % count) for i in range(count)])  8.36 us
    mul x3, other arithmetic, per_device(): extend_padded * ((inside_rows >= 0) & (inside_rows < total_rows)).astype(...  6.64 us
    another operation x3, local copies, waits for them, and re-layouts, from_root(): jnp.stack([own] * axis_size(axis))  5.58 us
    ppermute x6, starting transfers between devices, padded_2(): lax.ppermute(head, axis, [((i + 1) % count, i) for i in range(count)])  5.21 us
  transfers between devices with their start and end apart: 18, of which 12 were waited for; matrix products, arithmetic and copies ran while one was open for 8% of the time, Pallas kernels for 0%

profile of v1, /device:TPU:78, one launch (start us, length us, event | category | flops | bytes accessed | tf_op | source)
XLA Modules:
  0.0 177.4 jit_solution(18121609940832483084)
XLA Ops:
  6.5 0.8 fusion.114
  7.4 1.9 %broadcast_multiply_fusion = f32[8,16,32,128]{3,2,1,0:T(8,128)S(1)} fusion(f32[8,16,32,128]{3,2,1,0:T(8,128)} %param.9, f32[16,32,128]{2,1,0:T(8,128)S(1)} %fusion.114), kind=kLoop, calls=%fused_computation.189 | loop fusion | flops 524288 | bytes 4456448 | tf_op jit(solution)/shard_map/mul | solution.py:158
  9.3 1.0 slice_select_fusion.2
  10.5 4.5 %collective-permute-start = (f32[8,2,32,128]{3,2,1,0:T(8,128)S(1)}, f32[8,2,32,128]{3,2,1,0:T(8,128)S(1)}, u32[]{:S(2)}, u32[]{:S(2)}) collective-permute-start(f32[8,2,32,128]{3,2,1,0:T(8,128)S(1)} %get-tuple-element.152), channel_id=1, source_target_pairs={{0,4},{4,8},{8,12},{12,16},{16,20},{20,24},{24,28},{28,32},{32,36}... | collective-permute-start | bytes 786440 | tf_op jit(solution)/shard_map/ppermute | solution.py:25
  14.9 0.6 multiply_add_fusion.3
  15.5 20.0 %reduce-scatter.4.cloned.1.call-done = f32[384,128]{1,0:T(8,128)} async-done(((f32[1536,128]{1,0:T(8,128)}), f32[384,128]{1,0:T(8,128)}) %reduce-scatter.4.cloned.1.call-update) | async-done | bytes 196624 | tf_op jit(solution)/shard_map/reduce_scatter | solution.py:46
  35.5 1.8 %stack.18 = f32[4,384,128]{2,1,0:T(8,128)} broadcast(f32[384,128]{1,0:T(8,128)} %reduce-scatter.4.cloned.1.call-done), dimensions={1,2} | broadcast | bytes 983040 | tf_op jit(solution)/shard_map/stack | solution.py:47
  37.4 6.9 %all-to-all-start = ((f32[4,384,128]{2,1,0:T(8,128)}), f32[4,384,128]{2,1,0:T(8,128)}, u32[]{:S(2)}, u32[]{:S(2)}) async-start(f32[4,384,128]{2,1,0:T(8,128)} %stack.18), calls=%async_computation.1 | async-start | bytes 1572864 | tf_op jit(solution)/shard_map/all_to_all | solution.py:47
  44.6 1.7 collective-permute-start.3
  46.3 0.6 fusion.115
  47.0 2.4 %collective-permute-done.2 = f32[8,20,2,128]{3,2,1,0:T(2,128)S(1)} collective-permute-done((f32[8,20,2,128]{3,2,1,0:T(2,128)S(1)}, f32[8,20,2,128]{3,2,1,0:T(2,128)S(1)}, u32[]{:S(2)}, u32[]{:S(2)}) %collective-permute-start.2) | collective-permute-done | bytes 163872 | tf_op jit(solution)/shard_map/ppermute | solution.py:25
  49.3 0.7 copy-done.12
  50.1 2.3 %maximum_multiply_fusion = f32[8,20,36,128]{3,2,1,0:T(8,128)S(1)} fusion(f32[8,20,2,128]{3,2,1,0:T(2,128)} %collective-permute-done.3, f32[8,2,32,128]{3,2,1,0:T(8,128)} %copy-done.7, f32[8,16,32,128]{3,2,1,0:T(8,128)} %copy-done.2, f32[8,2,32,128]{3,2,1,0:T(8,128)} %copy-done.6, f32[8,20,2,128]{3,2,1,0:T(2,128)} %copy-done.12, f32[36]{0:T(128)S(1)} %and_convert_fusion), kind=kLoop, calls=%fused_computation.186 | loop fusion | flops 3686400 | bytes 5898384 | tf_op jit(solution)/shard_map/mul | solution.py:175
  52.4 1.3 all-to-all-done
  53.7 9.7 %conditional.3 = (f32[8,16,32,128]{3,2,1,0:T(8,128)S(1)}) conditional(s32[]{:T(128)} %convert_element_type.41, (f32[8,20,36,128]{3,2,1,0:T(8,128)S(1)}, f32[4,384,128]{2,1,0:T(8,128)}, f32[8,8]{1,0:T(8,128)S(1)}, f32[16,32,128]{2,1,0:T(8,128)S(1)}) %tuple.23, (f32[8,20,36,128]{3,2,1,0:T(8,128)S(1)}, f32[32]{0:T(128)S(1)}, f32[128,128]{1,0:T(8,128)}, ...), branch_computations={%region_1.2_spmd, %region_2.3_spmd} | conditional | flops 155859008 | bytes 41029640 | solution.py:170
  53.7 1.3 fusion.13
  55.0 1.7 copy.9
  56.8 6.1 %fusion.8 = f32[8,16,32,128]{3,0,2,1:T(8,128)S(1)} fusion(f32[8,16,32,128]{3,0,2,1:T(8,128)S(1)} %slice.573, f32[8,20,36,128]{3,0,2,1:T(8,128)S(1)} %copy.9, f32[16,32,128]{2,1,0:T(8,128)S(1)} %get-tuple-element.68, f32[16,32,128]{2,1,0:T(8,128)S(1)} %get-tuple-element.105, f32[16,32,128]{2,1,0:T(8,128)S(1)} %get-tuple-element.106, ...), kind=kOutput, calls=%fused_computation.10 | convolution fusion | flops 72351744 | bytes 24645632 | tf_op jit(solution)/shard_map/cond/branch_0_fun/ij,jxyz->ixyz/dot_general | solution.py:123
  63.4 1.0 slice_select_fusion.1
  64.5 3.5 %collective-permute-start.4 = (f32[8,2,32,128]{3,2,1,0:T(8,128)S(1)}, f32[8,2,32,128]{3,2,1,0:T(8,128)S(1)}, u32[]{:S(2)}, u32[]{:S(2)}) collective-permute-start(f32[8,2,32,128]{3,2,1,0:T(8,128)S(1)} %get-tuple-element.150), channel_id=1, source_target_pairs={{0,4},{4,8},{8,12},{12,16},{16,20},{20,24},{24,28},{28,32},{32,36}... | collective-permute-start | bytes 786440 | tf_op jit(solution)/shard_map/ppermute | solution.py:25
  68.1 20.4 %reduce-scatter.6.cloned.1.call-done = f32[384,128]{1,0:T(8,128)} async-done(((f32[1536,128]{1,0:T(8,128)}), f32[384,128]{1,0:T(8,128)}) %reduce-scatter.6.cloned.1.call-update) | async-done | bytes 196624 | tf_op jit(solution)/shard_map/reduce_scatter | solution.py:46
  88.5 1.9 %stack.22 = f32[4,384,128]{2,1,0:T(8,128)} broadcast(f32[384,128]{1,0:T(8,128)} %reduce-scatter.6.cloned.1.call-done), dimensions={1,2} | broadcast | bytes 983040 | tf_op jit(solution)/shard_map/stack | solution.py:47
  90.3 7.0 %all-to-all-start.1 = ((f32[4,384,128]{2,1,0:T(8,128)}), f32[4,384,128]{2,1,0:T(8,128)}, u32[]{:S(2)}, u32[]{:S(2)}) async-start(f32[4,384,128]{2,1,0:T(8,128)} %stack.22), calls=%async_computation.3 | async-start | bytes 1572864 | tf_op jit(solution)/shard_map/all_to_all | solution.py:47
  97.6 1.7 collective-permute-start.7
  99.3 3.0 %collective-permute-done.6 = f32[8,20,2,128]{3,2,1,0:T(2,128)S(1)} collective-permute-done((f32[8,20,2,128]{3,2,1,0:T(2,128)S(1)}, f32[8,20,2,128]{3,2,1,0:T(2,128)S(1)}, u32[]{:S(2)}, u32[]{:S(2)}) %collective-permute-start.6) | collective-permute-done | bytes 163872 | tf_op jit(solution)/shard_map/ppermute | solution.py:25
  102.3 0.8 collective-permute-done.7
  103.1 2.2 %maximum_multiply_fusion.1 = f32[8,20,36,128]{3,2,1,0:T(8,128)S(1)} fusion(f32[8,20,2,128]{3,2,1,0:T(2,128)S(1)} %collective-permute-done.7, f32[8,2,32,128]{3,2,1,0:T(8,128)} %copy-done.10, f32[8,16,32,128]{3,2,1,0:T(8,128)} %copy-done.3, f32[8,2,32,128]{3,2,1,0:T(8,128)} %copy-done.8, f32[8,20,2,128]{3,2,1,0:T(2,128)S(1)} %collective-permute-done.6, ...), kind=kLoop, calls=%fused_computation.187 | loop fusion | flops 3686400 | bytes 5898384 | tf_op jit(solution)/shard_map/mul | solution.py:175
  105.3 1.1 all-to-all-done.1
  106.4 9.7 %conditional.4 = (f32[8,16,32,128]{3,2,1,0:T(8,128)S(1)}) conditional(s32[]{:T(128)} %convert_element_type.41, (f32[8,20,36,128]{3,2,1,0:T(8,128)S(1)}, f32[4,384,128]{2,1,0:T(8,128)}, f32[8,8]{1,0:T(8,128)S(1)}, f32[16,32,128]{2,1,0:T(8,128)S(1)}) %tuple.25, (f32[8,20,36,128]{3,2,1,0:T(8,128)S(1)}, f32[32]{0:T(128)S(1)}, f32[128,128]{1,0:T(8,128)}, ...), branch_computations={%region_4.5_spmd, %region_5.6_spmd} | conditional | flops 155859008 | bytes 41029640 | solution.py:170
  106.4 1.3 fusion.51
  107.7 1.7 copy.10
  109.5 6.1 %fusion.46 = f32[8,16,32,128]{3,0,2,1:T(8,128)S(1)} fusion(f32[8,16,32,128]{3,0,2,1:T(8,128)S(1)} %slice.596, f32[8,20,36,128]{3,0,2,1:T(8,128)S(1)} %copy.10, f32[16,32,128]{2,1,0:T(8,128)S(1)} %get-tuple-element.76, f32[16,32,128]{2,1,0:T(8,128)S(1)} %get-tuple-element.118, f32[16,32,128]{2,1,0:T(8,128)S(1)} %get-tuple-element.119, ...), kind=kOutput, calls=%fused_computation.72 | convolution fusion | flops 72351744 | bytes 24645632 | tf_op jit(solution)/shard_map/cond/branch_0_fun/ij,jxyz->ixyz/dot_general | solution.py:123
  116.1 1.0 slice_select_fusion
  117.2 3.8 %collective-permute-start.8 = (f32[8,2,32,128]{3,2,1,0:T(8,128)S(1)}, f32[8,2,32,128]{3,2,1,0:T(8,128)S(1)}, u32[]{:S(2)}, u32[]{:S(2)}) collective-permute-start(f32[8,2,32,128]{3,2,1,0:T(8,128)S(1)} %get-tuple-element.148), channel_id=1, source_target_pairs={{0,4},{4,8},{8,12},{12,16},{16,20},{20,24},{24,28},{28,32},{32,36}... | collective-permute-start | bytes 786440 | tf_op jit(solution)/shard_map/ppermute | solution.py:25
  121.0 20.3 %reduce-scatter.8.cloned.1.call-done = f32[384,128]{1,0:T(8,128)} async-done(((f32[1536,128]{1,0:T(8,128)}), f32[384,128]{1,0:T(8,128)}) %reduce-scatter.8.cloned.1.call-update) | async-done | bytes 196624 | tf_op jit(solution)/shard_map/reduce_scatter | solution.py:46
  141.3 1.8 %stack.23 = f32[4,384,128]{2,1,0:T(8,128)} broadcast(f32[384,128]{1,0:T(8,128)} %reduce-scatter.8.cloned.1.call-done), dimensions={1,2} | broadcast | bytes 983040 | tf_op jit(solution)/shard_map/stack | solution.py:47
  143.1 7.0 %all-to-all-start.2 = ((f32[4,384,128]{2,1,0:T(8,128)}), f32[4,384,128]{2,1,0:T(8,128)}, u32[]{:S(2)}, u32[]{:S(2)}) async-start(f32[4,384,128]{2,1,0:T(8,128)} %stack.23), calls=%async_computation.5 | async-start | bytes 1572864 | tf_op jit(solution)/shard_map/all_to_all | solution.py:47
  150.4 1.7 collective-permute-start.11
  152.1 3.0 %collective-permute-done.10 = f32[8,20,2,128]{3,2,1,0:T(2,128)S(1)} collective-permute-done((f32[8,20,2,128]{3,2,1,0:T(2,128)S(1)}, f32[8,20,2,128]{3,2,1,0:T(2,128)S(1)}, u32[]{:S(2)}, u32[]{:S(2)}) %collective-permute-start.10) | collective-permute-done | bytes 163872 | tf_op jit(solution)/shard_map/ppermute | solution.py:25
  155.1 0.8 collective-permute-done.11
  155.9 2.2 %maximum_multiply_fusion.2 = f32[8,20,36,128]{3,2,1,0:T(8,128)S(1)} fusion(f32[8,20,2,128]{3,2,1,0:T(2,128)S(1)} %collective-permute-done.11, f32[8,2,32,128]{3,2,1,0:T(8,128)} %copy-done.11, f32[8,16,32,128]{3,2,1,0:T(8,128)} %copy-done.4, f32[8,2,32,128]{3,2,1,0:T(8,128)} %copy-done.9, f32[8,20,2,128]{3,2,1,0:T(2,128)S(1)} %collective-permute-done.10, ...), kind=kLoop, calls=%fused_computation.188 | loop fusion | flops 3686400 | bytes 5898384 | tf_op jit(solution)/shard_map/mul | solution.py:175
  158.1 1.0 all-to-all-done.2
  159.2 9.7 %conditional.5 = (f32[8,16,32,128]{3,2,1,0:T(8,128)S(1)}) conditional(s32[]{:T(128)} %convert_element_type.41, (f32[8,20,36,128]{3,2,1,0:T(8,128)S(1)}, f32[4,384,128]{2,1,0:T(8,128)}, f32[8,8]{1,0:T(8,128)S(1)}, f32[16,32,128]{2,1,0:T(8,128)S(1)}) %tuple.27, (f32[8,20,36,128]{3,2,1,0:T(8,128)S(1)}, f32[32]{0:T(128)S(1)}, f32[128,128]{1,0:T(8,128)}, ...), branch_computations={%region_7.8_spmd, %region_8.9_spmd} | conditional | flops 155859008 | bytes 41029640 | solution.py:170
  159.2 1.3 fusion.89
  160.4 1.7 copy.11
  162.3 6.1 %fusion.84 = f32[8,16,32,128]{3,0,2,1:T(8,128)S(1)} fusion(f32[8,16,32,128]{3,0,2,1:T(8,128)S(1)} %slice.619, f32[8,20,36,128]{3,0,2,1:T(8,128)S(1)} %copy.11, f32[16,32,128]{2,1,0:T(8,128)S(1)} %get-tuple-element.84, f32[16,32,128]{2,1,0:T(8,128)S(1)} %get-tuple-element.131, f32[16,32,128]{2,1,0:T(8,128)S(1)} %get-tuple-element.132, ...), kind=kOutput, calls=%fused_computation.134 | convolution fusion | flops 72351744 | bytes 24645632 | tf_op jit(solution)/shard_map/cond/branch_0_fun/ij,jxyz->ixyz/dot_general | solution.py:123
  168.9 1.3 copy-done.5
  170.2 0.7 copy-done.1
  (58 shorter events, 2.7 us)
Async XLA Ops:
  6.5 9.0 %copy-start = (f32[3,8,8]{2,1,0:T(8,128)S(1)}, f32[3,8,8]{2,1,0:T(8,128)}, u32[]{:S(2)}) copy-start(f32[3,8,8]{2,1,0:T(8,128)} %param.11) | copy-start | bytes 2308
  6.5 29.0 %reduce-scatter.4.cloned.1.call-start = ((), (), s32[]{:S(2)}) async-start(), calls=%async_computation.6 | async-start | bytes 983040 | tf_op jit(solution)/shard_map/reduce_scatter | solution.py:46
  9.3 35.0 %copy-start.2 = (f32[8,16,32,128]{3,2,1,0:T(8,128)}, f32[8,16,32,128]{3,2,1,0:T(8,128)S(1)}, u32[]{:S(2)}) copy-start(f32[8,16,32,128]{3,2,1,0:T(8,128)S(1)} %broadcast_multiply_fusion) | copy-start | bytes 6291460
  10.5 33.9 %collective-permute-start = (f32[8,2,32,128]{3,2,1,0:T(8,128)S(1)}, f32[8,2,32,128]{3,2,1,0:T(8,128)S(1)}, u32[]{:S(2)}, u32[]{:S(2)}) collective-permute-start(f32[8,2,32,128]{3,2,1,0:T(8,128)S(1)} %get-tuple-element.152), channel_id=1, source_target_pairs={{0,4},{4,8},{8,12},{12,16},{16,20},{20,24},{24,28},{28,32},{32,36}... | collective-permute-start | bytes 786440 | tf_op jit(solution)/shard_map/ppermute | solution.py:25
  14.9 29.4 %collective-permute-start.1 = (f32[8,2,32,128]{3,2,1,0:T(8,128)S(1)}, f32[8,2,32,128]{3,2,1,0:T(8,128)S(1)}, u32[]{:S(2)}, u32[]{:S(2)}) collective-permute-start(f32[8,2,32,128]{3,2,1,0:T(8,128)S(1)} %get-tuple-element.153), channel_id=1, source_target_pairs={{4,0},{8,4},{12,8},{16,12},{20,16},{24,20},{28,24},{32,28},{36,32}... | collective-permute-start | bytes 786440 | tf_op jit(solution)/shard_map/ppermute | solution.py:27
  37.4 16.3 %all-to-all-start = ((f32[4,384,128]{2,1,0:T(8,128)}), f32[4,384,128]{2,1,0:T(8,128)}, u32[]{:S(2)}, u32[]{:S(2)}) async-start(f32[4,384,128]{2,1,0:T(8,128)} %stack.18), calls=%async_computation.1 | async-start | bytes 1572864 | tf_op jit(solution)/shard_map/all_to_all | solution.py:47
  44.3 44.1 %reduce-scatter.6.cloned.1.call-start = ((), (), s32[]{:S(2)}) async-start(), calls=%async_computation.7 | async-start | bytes 983040 | tf_op jit(solution)/shard_map/reduce_scatter | solution.py:46
  44.3 5.0 %copy-start.6 = (f32[8,2,32,128]{3,2,1,0:T(8,128)}, f32[8,2,32,128]{3,2,1,0:T(8,128)S(1)}, u32[]{:S(2)}) copy-start(f32[8,2,32,128]{3,2,1,0:T(8,128)S(1)} %collective-permute-done) | copy-start | bytes 786436
  44.4 5.0 %copy-start.7 = (f32[8,2,32,128]{3,2,1,0:T(8,128)}, f32[8,2,32,128]{3,2,1,0:T(8,128)S(1)}, u32[]{:S(2)}) copy-start(f32[8,2,32,128]{3,2,1,0:T(8,128)S(1)} %collective-permute-done.1) | copy-start | bytes 786436
  44.5 4.8 %collective-permute-start.2 = (f32[8,20,2,128]{3,2,1,0:T(2,128)S(1)}, f32[8,20,2,128]{3,2,1,0:T(2,128)S(1)}, u32[]{:S(2)}, u32[]{:S(2)}) collective-permute-start(f32[8,20,2,128]{3,2,1,0:T(2,128)S(1)} %get-tuple-element.146), channel_id=1, source_target_pairs={{0,1},{1,2},{2,3},{3,0},{4,5},{5,6},{6,7},{7,4},{8,9},{9,10},{10,1... | collective-permute-start | bytes 491528 | tf_op jit(solution)/shard_map/ppermute | solution.py:25
  44.6 5.6 %collective-permute-start.3 = (f32[8,20,2,128]{3,2,1,0:T(2,128)S(1)}, f32[8,20,2,128]{3,2,1,0:T(2,128)}, u32[]{:S(2)}, u32[]{:S(2)}) collective-permute-start(f32[8,20,2,128]{3,2,1,0:T(2,128)S(1)} %get-tuple-element.147), channel_id=1, source_target_pairs={{1,0},{2,1},{3,2},{0,3},{5,4},{6,5},{7,6},{4,7},{9,8},{10,9},{11,1... | collective-permute-start | bytes 491528 | tf_op jit(solution)/shard_map/ppermute | solution.py:27
  46.9 6.7 %copy-start.13 = (f32[32]{0:T(128)S(1)}, f32[32]{0:T(128)}, u32[]{:S(2)}) copy-start(f32[32]{0:T(128)} %multiply_add_fusion.3) | copy-start | bytes 388
  49.3 0.7 copy-start.12
  63.4 34.0 %copy-start.3 = (f32[8,16,32,128]{3,2,1,0:T(8,128)}, f32[8,16,32,128]{3,2,1,0:T(8,128)S(1)}, u32[]{:S(2)}) copy-start(f32[8,16,32,128]{3,2,1,0:T(8,128)S(1)} %get-tuple-element.156) | copy-start | bytes 6291460
  64.5 32.8 %collective-permute-start.4 = (f32[8,2,32,128]{3,2,1,0:T(8,128)S(1)}, f32[8,2,32,128]{3,2,1,0:T(8,128)S(1)}, u32[]{:S(2)}, u32[]{:S(2)}) collective-permute-start(f32[8,2,32,128]{3,2,1,0:T(8,128)S(1)} %get-tuple-element.150), channel_id=1, source_target_pairs={{0,4},{4,8},{8,12},{12,16},{16,20},{20,24},{24,28},{28,32},{32,36}... | collective-permute-start | bytes 786440 | tf_op jit(solution)/shard_map/ppermute | solution.py:25
  68.1 29.3 %collective-permute-start.5 = (f32[8,2,32,128]{3,2,1,0:T(8,128)S(1)}, f32[8,2,32,128]{3,2,1,0:T(8,128)S(1)}, u32[]{:S(2)}, u32[]{:S(2)}) collective-permute-start(f32[8,2,32,128]{3,2,1,0:T(8,128)S(1)} %get-tuple-element.151), channel_id=1, source_target_pairs={{4,0},{8,4},{12,8},{16,12},{20,16},{24,20},{28,24},{32,28},{36,32}... | collective-permute-start | bytes 786440 | tf_op jit(solution)/shard_map/ppermute | solution.py:27
  90.3 16.0 %all-to-all-start.1 = ((f32[4,384,128]{2,1,0:T(8,128)}), f32[4,384,128]{2,1,0:T(8,128)}, u32[]{:S(2)}, u32[]{:S(2)}) async-start(f32[4,384,128]{2,1,0:T(8,128)} %stack.22), calls=%async_computation.3 | async-start | bytes 1572864 | tf_op jit(solution)/shard_map/all_to_all | solution.py:47
  97.3 44.0 %reduce-scatter.8.cloned.1.call-start = ((), (), s32[]{:S(2)}) async-start(), calls=%async_computation.8 | async-start | bytes 983040 | tf_op jit(solution)/shard_map/reduce_scatter | solution.py:46
  97.3 5.0 %copy-start.8 = (f32[8,2,32,128]{3,2,1,0:T(8,128)}, f32[8,2,32,128]{3,2,1,0:T(8,128)S(1)}, u32[]{:S(2)}) copy-start(f32[8,2,32,128]{3,2,1,0:T(8,128)S(1)} %collective-permute-done.4) | copy-start | bytes 786436
  97.4 5.0 %copy-start.10 = (f32[8,2,32,128]{3,2,1,0:T(8,128)}, f32[8,2,32,128]{3,2,1,0:T(8,128)S(1)}, u32[]{:S(2)}) copy-start(f32[8,2,32,128]{3,2,1,0:T(8,128)S(1)} %collective-permute-done.5) | copy-start | bytes 786436
  97.5 4.8 %collective-permute-start.6 = (f32[8,20,2,128]{3,2,1,0:T(2,128)S(1)}, f32[8,20,2,128]{3,2,1,0:T(2,128)S(1)}, u32[]{:S(2)}, u32[]{:S(2)}) collective-permute-start(f32[8,20,2,128]{3,2,1,0:T(2,128)S(1)} %get-tuple-element.144), channel_id=1, source_target_pairs={{0,1},{1,2},{2,3},{3,0},{4,5},{5,6},{6,7},{7,4},{8,9},{9,10},{10,1... | collective-permute-start | bytes 491528 | tf_op jit(solution)/shard_map/ppermute | solution.py:25
  97.6 5.6 %collective-permute-start.7 = (f32[8,20,2,128]{3,2,1,0:T(2,128)S(1)}, f32[8,20,2,128]{3,2,1,0:T(2,128)S(1)}, u32[]{:S(2)}, u32[]{:S(2)}) collective-permute-start(f32[8,20,2,128]{3,2,1,0:T(2,128)S(1)} %get-tuple-element.145), channel_id=1, source_target_pairs={{1,0},{2,1},{3,2},{0,3},{5,4},{6,5},{7,6},{4,7},{9,8},{10,9},{11,1... | collective-permute-start | bytes 491528 | tf_op jit(solution)/shard_map/ppermute | solution.py:27
  116.1 34.0 %copy-start.4 = (f32[8,16,32,128]{3,2,1,0:T(8,128)}, f32[8,16,32,128]{3,2,1,0:T(8,128)S(1)}, u32[]{:S(2)}) copy-start(f32[8,16,32,128]{3,2,1,0:T(8,128)S(1)} %get-tuple-element.157) | copy-start | bytes 6291460
  117.2 32.9 %collective-permute-start.8 = (f32[8,2,32,128]{3,2,1,0:T(8,128)S(1)}, f32[8,2,32,128]{3,2,1,0:T(8,128)S(1)}, u32[]{:S(2)}, u32[]{:S(2)}) collective-permute-start(f32[8,2,32,128]{3,2,1,0:T(8,128)S(1)} %get-tuple-element.148), channel_id=1, source_target_pairs={{0,4},{4,8},{8,12},{12,16},{16,20},{20,24},{24,28},{28,32},{32,36}... | collective-permute-start | bytes 786440 | tf_op jit(solution)/shard_map/ppermute | solution.py:25
  121.0 29.1 %collective-permute-start.9 = (f32[8,2,32,128]{3,2,1,0:T(8,128)S(1)}, f32[8,2,32,128]{3,2,1,0:T(8,128)S(1)}, u32[]{:S(2)}, u32[]{:S(2)}) collective-permute-start(f32[8,2,32,128]{3,2,1,0:T(8,128)S(1)} %get-tuple-element.149), channel_id=1, source_target_pairs={{4,0},{8,4},{12,8},{16,12},{20,16},{24,20},{28,24},{32,28},{36,32}... | collective-permute-start | bytes 786440 | tf_op jit(solution)/shard_map/ppermute | solution.py:27
  143.1 16.0 %all-to-all-start.2 = ((f32[4,384,128]{2,1,0:T(8,128)}), f32[4,384,128]{2,1,0:T(8,128)}, u32[]{:S(2)}, u32[]{:S(2)}) async-start(f32[4,384,128]{2,1,0:T(8,128)} %stack.23), calls=%async_computation.5 | async-start | bytes 1572864 | tf_op jit(solution)/shard_map/all_to_all | solution.py:47
  150.1 5.0 %copy-start.9 = (f32[8,2,32,128]{3,2,1,0:T(8,128)}, f32[8,2,32,128]{3,2,1,0:T(8,128)S(1)}, u32[]{:S(2)}) copy-start(f32[8,2,32,128]{3,2,1,0:T(8,128)S(1)} %collective-permute-done.8) | copy-start | bytes 786436
  150.1 5.0 %copy-start.11 = (f32[8,2,32,128]{3,2,1,0:T(8,128)}, f32[8,2,32,128]{3,2,1,0:T(8,128)S(1)}, u32[]{:S(2)}) copy-start(f32[8,2,32,128]{3,2,1,0:T(8,128)S(1)} %collective-permute-done.9) | copy-start | bytes 786436
  150.3 4.8 %collective-permute-start.10 = (f32[8,20,2,128]{3,2,1,0:T(2,128)S(1)}, f32[8,20,2,128]{3,2,1,0:T(2,128)S(1)}, u32[]{:S(2)}, u32[]{:S(2)}) collective-permute-start(f32[8,20,2,128]{3,2,1,0:T(2,128)S(1)} %get-tuple-element.142), channel_id=1, source_target_pairs={{0,1},{1,2},{2,3},{3,0},{4,5},{5,6},{6,7},{7,4},{8,9},{9,10},{10,1... | collective-permute-start | bytes 491528 | tf_op jit(solution)/shard_map/ppermute | solution.py:25
  150.4 5.6 %collective-permute-start.11 = (f32[8,20,2,128]{3,2,1,0:T(2,128)S(1)}, f32[8,20,2,128]{3,2,1,0:T(2,128)S(1)}, u32[]{:S(2)}, u32[]{:S(2)}) collective-permute-start(f32[8,20,2,128]{3,2,1,0:T(2,128)S(1)} %get-tuple-element.143), channel_id=1, source_target_pairs={{1,0},{2,1},{3,2},{0,3},{5,4},{6,5},{7,6},{4,7},{9,8},{10,9},{11,1... | collective-permute-start | bytes 491528 | tf_op jit(solution)/shard_map/ppermute | solution.py:27
  168.9 1.3 copy-start.5
  170.2 0.7 copy-start.1
Sparse Core Ops, SparseCore 0:
  10.5 24.9 reduce-scatter.3
  64.6 23.8 reduce-scatter.5
  117.3 23.9 reduce-scatter.7
